TPU v7x, 32 devices: a whole 2x2x4 slice. The times are simulated.
32 devices in a mesh: shard: 8 (over z, x), replica: 4 (over y, core).
Axes of the slice: x: 2, y: 2, z: 4, core: 2. Of those that a mesh axis runs over, the one named last changes fastest.
Arguments:
- samples: bfloat16 [2048, 480, 128], P(('shard', 'replica')), may hold values from -6 to 6
- counts: int32 [2048], P(('shard', 'replica')), may hold values from 1 to 480
- buckets: int32 [2048, 480], P(('shard', 'replica')), may hold values from 0 to 127
- block_series: int32 [2048], P(('shard', 'replica')), may hold values from 0 to 63, as said below
- owner_map: int32 [64], replicated, may hold values from 0 to 63
Outputs:
- cold_stats: float32 [8, 4, 128, 4, 8, 128], P('shard', 'replica')
- sketches: float32 [64, 128, 128], P(('shard', 'replica'))
- live_rows: float32 [64], P(('shard', 'replica'))
Inputs may be any that keep to these rules, and one draw needn't show every extreme that they name: `block_series`: owner_map is a permutation of 0 to 63. With owner = owner_map[series] // 8, the 64 blocks of one device name at most 16 blocks of any one owner, and in every draw some owner gets exactly 16 blocks from every device.
All inputs are finite; a program needn't handle non-finite values.
Results may differ from a plain program's by a relative error of at most 0.0003.
Values may be sent and summed in bfloat16 or wider, within the bound.
No kernel may reach another device: no remote copies, remote signals or barrier semaphores. Data moves between devices by JAX's collectives and lax.ppermute only.
A program may use at most 192 MiB of HBM per device.

v0:
```python
import jax
import jax.numpy as jnp
from jax import lax
from jax.sharding import PartitionSpec as P

BINS = 128


def minute_stats(values, counts):
    blocks, samples, lanes = values.shape
    minutes = samples // 60
    steps = jnp.arange(samples, dtype=jnp.int32)
    live = (steps[None, :] < counts[:, None]).reshape(blocks, minutes, 60, 1)
    data = values.astype(jnp.float32).reshape(blocks, minutes, 60, lanes)
    count = jnp.sum(jnp.where(live, jnp.float32(1.0), jnp.float32(0.0)), axis=2)
    count = jnp.broadcast_to(count, (blocks, minutes, lanes))
    total = jnp.sum(jnp.where(live, data, jnp.float32(0.0)), axis=2)
    lowest = jnp.min(jnp.where(live, data, jnp.inf), axis=2)
    highest = jnp.max(jnp.where(live, data, -jnp.inf), axis=2)
    filled = count > 0
    lowest = jnp.where(filled, lowest, jnp.float32(0.0))
    highest = jnp.where(filled, highest, jnp.float32(0.0))
    return jnp.stack([lowest, highest, total, count], axis=1)


def bucket_sketch(values, marks, counts):
    samples = values.shape[1]
    steps = lax.broadcasted_iota(jnp.int32, (1, 1, samples), 2)
    levels = lax.broadcasted_iota(jnp.int32, (1, BINS, 1), 1)
    table = ((marks[:, None, :] == levels) & (steps < counts[:, None, None])).astype(jnp.bfloat16)
    return jnp.einsum("nks,nsl->nkl", table, values, preferred_element_type=jnp.float32)


def body(samples, counts, buckets, block_series, owner_map):
    blocks = samples.shape[0]
    shards = lax.axis_size("shard")
    replicas = lax.axis_size("replica")
    cap = max(2, (2 * blocks + shards - 1) // shards)
    ser_own = owner_map.shape[0] // shards
    ser_dev = ser_own // replicas
    position = owner_map[block_series]
    owner = position // ser_own
    local = position % ser_own
    index = jnp.arange(blocks, dtype=jnp.int32)
    same = (owner[:, None] == owner[None, :]) & (index[None, :] < index[:, None])
    rank = jnp.sum(same.astype(jnp.int32), axis=1)
    slot = owner * cap + rank
    match = slot[:, None] == jnp.arange(shards * cap, dtype=jnp.int32)[None, :]
    source = jnp.sum(jnp.where(match, index[:, None], 0), axis=0)
    used = jnp.any(match, axis=0)
    series_levels = jnp.arange(ser_own, dtype=jnp.int32)
    stats_all = minute_stats(samples, counts)
    sketch_all = bucket_sketch(samples, buckets, counts)
    stats_buf = jnp.where(used[:, None, None, None], stats_all[source], 0.0)
    stats_buf = stats_buf.reshape((shards, cap) + stats_all.shape[1:])
    sketch_buf = jnp.where(used[:, None, None], sketch_all[source], 0.0)
    sketch_buf = sketch_buf.reshape((shards, cap) + sketch_all.shape[1:])
    place_buf = jnp.where(
        used[:, None], (local[source][:, None] == series_levels).astype(jnp.float32), 0.0
    )
    place_buf = place_buf.reshape(shards, cap, ser_own)
    rows_buf = jnp.where(used, counts[source], 0).astype(jnp.float32).reshape(shards, cap)
    stats, sketch, place, rows = (
        lax.all_to_all(stats_buf, "shard", split_axis=0, concat_axis=0, tiled=True),
        lax.all_to_all(sketch_buf, "shard", split_axis=0, concat_axis=0, tiled=True),
        lax.all_to_all(place_buf, "shard", split_axis=0, concat_axis=0, tiled=True),
        lax.all_to_all(rows_buf, "shard", split_axis=0, concat_axis=0, tiled=True),
    )
    series_sketch = jnp.einsum("sck,scbl->kbl", place, sketch, precision=lax.Precision.HIGHEST)
    series_rows = jnp.einsum("sck,sc->k", place, rows, precision=lax.Precision.HIGHEST)
    whole_sketch, whole_rows = lax.psum((series_sketch, series_rows), "replica")
    start = lax.axis_index("replica") * ser_dev
    sketches = lax.dynamic_slice_in_dim(whole_sketch, start, ser_dev, 0)
    live_rows = lax.dynamic_slice_in_dim(whole_rows, start, ser_dev, 0)
    cold_stats = stats.reshape((1, 1, shards * cap) + stats.shape[2:])
    return (cold_stats, sketches, live_rows)


def solution(mesh):
    return jax.shard_map(
        body,
        mesh=mesh,
        in_specs=(
            P(("shard", "replica"), None, None),
            P(("shard", "replica")),
            P(("shard", "replica"), None),
            P(("shard", "replica")),
            P(),
        ),
        out_specs=(
            P("shard", "replica", None, None, None, None),
            P(("shard", "replica"), None, None),
            P(("shard", "replica")),
        ),
        check_vma=False,
    )
```

profile of v0, /device:TPU:0, one launch (start us, length us, event | category | flops | bytes accessed | tf_op | source)
XLA Modules:
  0.0 316.9 jit_solution(14696365018628857801)
XLA Ops:
  7.2 0.0 copy-start
  7.2 0.7 compare_select_fusion.1
  7.9 0.8 gather_fusion
  8.6 0.2 convert_reduce_fusion
  8.8 0.1 select_reduce_fusion.1
  8.9 0.1 fusion.9
  9.1 1.6 gather_fusion.4
  10.6 0.7 convert_element_type.26
  11.3 7.3 %all-to-all-start.3 = ((f32[8,1,16]{2,1,0:T(1,128)}), f32[8,1,16]{2,1,0:T(1,128)S(1)}, u32[]{:S(2)}, u32[]{:S(2)}) async-start(f32[8,1,16]{2,1,0:T(1,128)} %bitcast.13), calls=%async_computation.3 | async-start | bytes 8192 | tf_op jit(solution)/shard_map/all_to_all | solution.py:67
  18.6 0.1 broadcast_in_dim.120
  18.7 0.7 iota_compare_fusion.1
  19.5 1.2 gather_fusion.2
  20.7 0.1 eq.63
  20.8 18.5 %fusion.4 = f32[64,128,128]{2,1,0:T(8,128)} fusion(bf16[64,480,128]{2,1,0:T(8,128)(2,1)} %param.5, s32[64,480]{1,0:T(8,128)} %param.7, pred[64,480]{1,0:T(8,128)(4,1)S(1)} %iota_compare_fusion.1), kind=kOutput, calls=%fused_computation.13 | convolution fusion | flops 1014497280 | bytes 12212224 | tf_op jit(solution)/shard_map/nks,nsl->nkl/dot_general | solution.py:31
  39.3 0.7 reshape.256
  40.0 6.5 %gather_fusion.3 = f32[128,128,128]{2,1,0:T(8,128)} fusion(f32[64,128,128]{2,1,0:T(8,128)} %fusion.4, s32[1024]{0:T(1024)S(1)} %pad_clamp_fusion), kind=kCustom, calls=%fused_computation.3 | custom fusion | bytes 16777728 | tf_op jit(solution)/shard_map/gather | solution.py:56
  46.5 6.0 %all-to-all-start.1 = ((f32[8,1,128]{2,1,0:T(1,128)}), f32[8,1,128]{2,1,0:T(1,128)S(1)}, u32[]{:S(2)}, u32[]{:S(2)}) async-start(f32[8,1,128]{2,1,0:T(1,128)} %reshape.256), calls=%async_computation.1 | async-start | bytes 8192 | tf_op jit(solution)/shard_map/all_to_all | solution.py:66
  52.5 12.3 %copy_select_fusion = f32[8,16,128,128]{3,1,2,0:T(8,128)} fusion(f32[8,16,128,128]{3,2,1,0:T(8,128)} %bitcast.47, pred[8,16]{1,0:T(8,128)(4,1)S(1)} %broadcast_in_dim.120), kind=kLoop, calls=%fused_computation.14 | loop fusion | flops 2097152 | bytes 16777344 | tf_op jit(solution)/shard_map/jit(_where)/select_n | solution.py:56
  64.8 6.0 %all-to-all-start.2 = ((f32[8,16,128,128]{3,1,2,0:T(8,128)}), f32[8,16,128,128]{3,1,2,0:T(8,128)}, u32[]{:S(2)}, u32[]{:S(2)}) async-start(f32[8,16,128,128]{3,1,2,0:T(8,128)} %copy_select_fusion), calls=%async_computation.2 | async-start | bytes 16777216 | tf_op jit(solution)/shard_map/all_to_all | solution.py:65
  70.8 9.3 %copy.29 = bf16[64,480,128]{2,0,1:T(8,128)(2,1)} copy(bf16[64,480,128]{2,1,0:T(8,128)(2,1)} %param.5) | data formatting | bytes 15728640 | tf_op args[0]
  80.2 0.1 copy.28
  80.3 0.1 select_reduce_fusion
  80.4 0.1 copy.33
  80.5 0.1 copy.27
  80.6 0.1 broadcast_compare_fusion
  80.7 8.5 %fusion = (f32[64,8,128]{2,0,1:T(8,128)S(1)}, f32[64,8,128]{2,0,1:T(8,128)S(1)}, f32[64,8,128]{2,0,1:T(8,128)S(1)}) fusion(bf16[64,8,60,128]{3,0,2,1:T(8,128)(2,1)} %bitcast.48, pred[64,8,60]{0,2,1:T(8,128)(4,1)S(1)} %broadcast_compare_fusion), kind=kLoop, calls=%fused_computation.8 | loop fusion | flops 27328512 | bytes 8681472 | tf_op jit(solution)/shard_map/reduce_min | solution.py:18
  89.3 0.2 copy.44
  89.4 0.4 bitcast_select_fusion.1
  89.8 0.1 stack_broadcast_in_dim.2
  89.9 0.1 pad_maximum_fusion
  90.0 0.8 gather_fusion.1
  90.8 1.5 broadcast_select_fusion
  92.3 160.5 %all-to-all-done.2 = f32[8,16,128,128]{3,1,2,0:T(8,128)} async-done(((f32[8,16,128,128]{3,1,2,0:T(8,128)}), f32[8,16,128,128]{3,1,2,0:T(8,128)}, u32[]{:S(2)}, u32[]{:S(2)}) %all-to-all-start.2) | async-done | bytes 8388640 | tf_op jit(solution)/shard_map/all_to_all | solution.py:65
  252.9 3.6 %all-to-all-start = ((f32[8,16,4,8,128]{4,3,2,1,0:T(8,128)}), f32[8,16,4,8,128]{4,3,2,1,0:T(8,128)S(1)}, u32[]{:S(2)}, u32[]{:S(2)}) async-start(f32[8,16,4,8,128]{4,3,2,1,0:T(8,128)} %broadcast_select_fusion), calls=%async_computation | async-start | bytes 4194304 | tf_op jit(solution)/shard_map/all_to_all | solution.py:64
  256.5 0.0 all-reduce.2.cloned.1.call-start
  256.6 0.5 broadcast.250
  257.1 0.7 reduce.1
  257.7 0.1 reshape.257
  257.8 14.2 %convolution_bitcast_fusion = f32[8,128,128]{2,0,1:T(8,128)} fusion(f32[8,16,128,128]{3,1,2,0:T(8,128)} %all-to-all-done.2, f32[8,8,16]{2,1,0:T(8,128)S(1)} %reshape.257), kind=kOutput, calls=%fused_computation.17 | convolution fusion | flops 201326592 | bytes 8916992 | tf_op jit(solution)/shard_map/sck,scbl->kbl/dot_general | solution.py:69
  272.0 0.0 all-reduce.2.cloned.1.call-update
  272.0 0.2 convolution_bitcast_fusion.1
  272.2 6.8 %psum.15 = f32[8]{0:T(128)S(1)} all-reduce(f32[8]{0:T(128)S(1)} %convolution_bitcast_fusion.1), channel_id=1, replica_groups=mesh['shard'=8,'replica'=4] {'replica'}, use_global_device_ids=true, to_apply=%region_8.9 | all-reduce | flops 8 | bytes 64 | tf_op jit(solution)/shard_map/psum | solution.py:71
  279.0 0.6 dynamic_slice.7
  279.6 25.4 %all-to-all-done = f32[8,16,4,8,128]{4,3,2,1,0:T(8,128)S(1)} async-done(((f32[8,16,4,8,128]{4,3,2,1,0:T(8,128)}), f32[8,16,4,8,128]{4,3,2,1,0:T(8,128)S(1)}, u32[]{:S(2)}, u32[]{:S(2)}) %all-to-all-start) | async-done | bytes 2097184 | tf_op jit(solution)/shard_map/all_to_all | solution.py:64
  304.9 2.1 all-reduce.2.cloned.1.call-done
  307.0 1.1 constant_dynamic-slice_fusion
  308.1 0.7 copy.37
  308.8 1.3 copy.47
  (14 shorter events, 0.1 us)
Async XLA Ops:
  7.2 0.7 copy-start
  11.3 35.2 %all-to-all-start.3 = ((f32[8,1,16]{2,1,0:T(1,128)}), f32[8,1,16]{2,1,0:T(1,128)S(1)}, u32[]{:S(2)}, u32[]{:S(2)}) async-start(f32[8,1,16]{2,1,0:T(1,128)} %bitcast.13), calls=%async_computation.3 | async-start | bytes 8192 | tf_op jit(solution)/shard_map/all_to_all | solution.py:67
  46.5 18.3 %all-to-all-start.1 = ((f32[8,1,128]{2,1,0:T(1,128)}), f32[8,1,128]{2,1,0:T(1,128)S(1)}, u32[]{:S(2)}, u32[]{:S(2)}) async-start(f32[8,1,128]{2,1,0:T(1,128)} %reshape.256), calls=%async_computation.1 | async-start | bytes 8192 | tf_op jit(solution)/shard_map/all_to_all | solution.py:66
  64.8 188.0 %all-to-all-start.2 = ((f32[8,16,128,128]{3,1,2,0:T(8,128)}), f32[8,16,128,128]{3,1,2,0:T(8,128)}, u32[]{:S(2)}, u32[]{:S(2)}) async-start(f32[8,16,128,128]{3,1,2,0:T(8,128)} %copy_select_fusion), calls=%async_computation.2 | async-start | bytes 16777216 | tf_op jit(solution)/shard_map/all_to_all | solution.py:65
  70.8 9.4 %copy-start.1 = (s32[64]{0:T(128)S(1)}, s32[64]{0:T(128)}, u32[]{:S(2)}) copy-start(s32[64]{0:T(128)} %param.6) | copy-start | bytes 772
  252.9 52.1 %all-to-all-start = ((f32[8,16,4,8,128]{4,3,2,1,0:T(8,128)}), f32[8,16,4,8,128]{4,3,2,1,0:T(8,128)S(1)}, u32[]{:S(2)}, u32[]{:S(2)}) async-start(f32[8,16,4,8,128]{4,3,2,1,0:T(8,128)} %broadcast_select_fusion), calls=%async_computation | async-start | bytes 4194304 | tf_op jit(solution)/shard_map/all_to_all | solution.py:64
  256.5 50.5 %all-reduce.2.cloned.1.call-start = ((), (), s32[]{:S(2)}) async-start(), calls=%async_computation.4 | async-start | bytes 1048576 | tf_op jit(solution)/shard_map/psum | solution.py:71
Sparse Core Ops, SparseCore 0:
  272.1 34.8 all-reduce.1
where the time goes:
time: 318 us; the launch traced here: 317 us
  waiting for transfers between devices  188 us (59%)
  matrix products  32.9 us (10%)
  local copies, waits for them, and re-layouts  26.5 us (8%)
  other arithmetic  25.6 us (8%)
  starting transfers between devices  23 us (7%)
  between operations  14.2 us (4%)
  blocking collectives  6.8 us (2%)
    all_to_all x1, waiting for transfers between devices, body(): lax.all_to_all(sketch_buf, 'shard', split_axis=0, concat_axis=0, tiled=True)  161 us
    all_to_all x1, waiting for transfers between devices, body(): lax.all_to_all(stats_buf, 'shard', split_axis=0, concat_axis=0, tiled=True)  25.4 us
    dot_general x1, matrix products, bucket_sketch(): jnp.einsum('nks,nsl->nkl', table, values, preferred_element_type=jnp.floa...  18.5 us
    dot_general x1, matrix products, body(): jnp.einsum('sck,scbl->kbl', place, sketch, precision=lax.Precision.HIGHEST)  14.2 us
    select_n x1, other arithmetic, body(): sketch_buf = jnp.where(used[:, None, None], sketch_all[source], 0.0)  12.3 us
    unnamed x9, local copies, waits for them, and re-layouts  12.1 us
    reduce_min x1, other arithmetic, minute_stats(): lowest = jnp.min(jnp.where(live, data, jnp.inf), axis=2)  8.5 us
    all_to_all x1, starting transfers between devices, body(): lax.all_to_all(rows_buf, 'shard', split_axis=0, concat_axis=0, tiled=True)  7.28 us
  transfers between devices with their start and end apart: 5, of which 3 were waited for; matrix products, arithmetic and copies ran while one was open for 25% of the time, Pallas kernels for 0%

commit v1 on v0

v1 whole, which is shorter than its diff:
```python
import functools

import jax
import jax.numpy as jnp
from jax import lax
from jax.experimental import pallas as pl
from jax.experimental.pallas import tpu as pltpu
from jax.sharding import PartitionSpec as P

BINS = 128
MINUTE = 60
SUB = 8
PACK = 16
LIMIT = 6.0
STEPS16 = 32767.0
LIVE_BASE = 16384
VMEM_LIMIT = 56 * 2**20

ANY = pl.BlockSpec(memory_space=pl.ANY)
SMEM = pl.BlockSpec(memory_space=pltpu.SMEM)
VMEM = pl.BlockSpec(memory_space=pltpu.VMEM)


def round_up(n, m):
    return -(-n // m) * m


def to_int16(x):
    return jnp.floor(x + 0.5).astype(jnp.int32).astype(jnp.int16)


class Plan:
    def __init__(self, shards, replicas, series, blocks):
        self.shards, self.replicas, self.series = shards, replicas, series
        self.ser_own = series // shards
        self.ser_dev = self.ser_own // replicas
        self.cap = max(2, (2 * blocks + shards - 1) // shards)
        self.rest = (replicas // 2) * shards
        self.bits = self.rest.bit_length() - 1
        self.half = self.rest * self.ser_dev
        sbits = shards.bit_length() - 1
        assert replicas >= 2 and 2**self.bits == self.rest
        self.order = list(range(sbits, self.bits)) + list(range(sbits))
        self.sum_at = self.cap * 2 * SUB
        self.count_at = self.sum_at + round_up(self.cap * SUB, PACK)
        self.pay_rows = self.count_at + round_up(self.cap, PACK)

    def partner(self, step):
        bit = -1 if step < 0 else self.order[step]
        sbits = self.shards.bit_length() - 1
        if step < 0:
            axis, size, flip = "replica", self.replicas, 1
        elif bit >= sbits:
            axis, size, flip = "replica", self.replicas, 2 << (bit - sbits)
        else:
            axis, size, flip = "shard", self.shards, 1 << bit
        return axis, [(i, i ^ flip) for i in range(size)]

    def count(self, step):
        return (1 << (self.bits - step - 1)) * self.ser_dev

    def rows(self, step):
        n = self.count(step)
        return n * BINS + round_up(n, PACK) + PACK

    def squeeze(self, j, steps):
        out, at = 0, 0
        for bit in range(self.bits):
            if bit not in self.order[:steps]:
                out = out + (((j >> bit) & 1) << at)
                at += 1
        return out

    def spread(self, index, steps):
        out, at = 0, 0
        for bit in range(self.bits):
            if bit not in self.order[:steps]:
                out |= ((index >> at) & 1) << bit
                at += 1
        return out


def reduce_rows(parts, op, row):
    out = list(parts)
    for width in (4, 2, 1):
        low = (row & width) == 0
        merged = []
        for i in range(width):
            a, b = out[i], out[i + width]
            first = jnp.where(low, a, b)
            other = jnp.where(low, b, a)
            up = pltpu.roll(other, SUB - width, 0)
            if width == 4:
                turned = up
            else:
                turned = jnp.where(low, up, pltpu.roll(other, width, 0))
            merged.append(op(first, turned))
        out = merged
    return out[0]


def minute_ends(x, count, minutes, op, worst, row16):
    lanes = x.shape[1]
    fill = jnp.full((PACK, lanes), worst, x.dtype)
    tiles = []
    for v in range(x.shape[0] // PACK):
        live = row16 < (count - PACK * v)
        tiles.append(jnp.where(live, x[PACK * v : PACK * (v + 1)], fill))
    out = []
    for m in range(minutes):
        lo, hi = m * MINUTE, (m + 1) * MINUTE
        total = None
        for v in range(lo // PACK, -(-hi // PACK)):
            tile = tiles[v]
            if v * PACK < lo:
                tile = jnp.where(row16 >= lo - v * PACK, tile, fill)
            if (v + 1) * PACK > hi:
                tile = jnp.where(row16 < hi - v * PACK, tile, fill)
            total = tile if total is None else op(total, tile)
        wide = total.astype(jnp.float32)
        out.append(op(wide[:SUB], wide[SUB:]))
    return out


def ingest_kernel(
    plan, counts, series, omap, buckets, samples, send, keep, pay_out,
    buf, acc, pay, sums, tallies, used, sem, out_sem,
):
    blocks, rows, lanes = buf.shape
    minutes = rows // MINUTE
    me = lax.axis_index("replica")
    copies = lambda b: pltpu.make_async_copy(samples.at[b], buf.at[b], sem.at[b])

    @pl.loop(0, blocks)
    def _(b):
        copies(b).start()

    for o in range(plan.shards):
        used[o] = 0
    tallies[...] = jnp.zeros_like(tallies)

    @pl.loop(0, 2 * plan.half)
    def _(i):
        acc[i] = jnp.zeros((BINS, lanes), jnp.float32)

    when = lax.broadcasted_iota(jnp.int32, (1, rows), 1)
    which = when // MINUTE
    levels = lax.broadcasted_iota(jnp.int32, (BINS + PACK, rows), 0)
    row = lax.broadcasted_iota(jnp.int32, (SUB, lanes), 0)
    row16 = lax.broadcasted_iota(jnp.int32, (PACK, lanes), 0)
    place = row * lanes + lax.broadcasted_iota(jnp.int32, (SUB, lanes), 1)

    def step(b, live_total):
        count = counts[b]
        p = omap[series[b]]
        o = p // plan.ser_own
        local = p - o * plan.ser_own
        r = local // plan.ser_dev
        d = local - r * plan.ser_dev
        c = used[o]
        used[o] = c + 1
        away = (r ^ me) & 1
        j = ((r >> 1) * plan.shards + o) * plan.ser_dev + d
        copies(b).wait()
        x = buf[b]
        live = when < count
        marks = jnp.where(live, buckets[pl.ds(b, 1), :], -1)
        whole = jnp.where(live, which, -1)
        marks = jnp.broadcast_to(marks, (BINS, rows))
        whole = jnp.broadcast_to(whole, (PACK, rows))
        hot = jnp.concatenate(
            [
                (marks == levels[:BINS]).astype(jnp.float32).astype(jnp.bfloat16),
                (whole == levels[:PACK]).astype(jnp.float32).astype(jnp.bfloat16),
            ],
            axis=0,
        )
        out = jnp.dot(hot, x, preferred_element_type=jnp.float32)
        at = away * plan.half + j
        acc[at] += out[:BINS]
        low = minute_ends(x, count, minutes, jnp.minimum, jnp.inf, row16)
        high = minute_ends(x, count, minutes, jnp.maximum, -jnp.inf, row16)
        low = reduce_rows(low, jnp.minimum, row)
        high = reduce_rows(high, jnp.maximum, row)
        n = jnp.clip(count - MINUTE * row, 0, MINUTE).astype(jnp.float32)
        filled = n > 0
        scale = STEPS16 / LIMIT
        ends = jnp.concatenate(
            [jnp.where(filled, low, 0.0), jnp.where(filled, high, 0.0)], axis=0
        )
        pay[o, pl.ds(pl.multiple_of(c * 2 * SUB, 2 * SUB), 2 * SUB), :] = to_int16(ends * scale)
        mean = out[BINS : BINS + SUB] / jnp.maximum(n, 1.0)
        mean = jnp.clip(mean, -LIMIT, LIMIT) * scale
        at8 = pl.multiple_of((o * plan.cap + c) * SUB, SUB)
        sums[pl.ds(at8, SUB), :] = jnp.floor(mean + 0.5).astype(jnp.int32)
        tallies[pl.ds(o * round_up(plan.cap, PACK) + c, 1), :] = jnp.full((1, lanes), count, jnp.int32)
        return live_total + jnp.where(place == p, count, 0)

    live_total = lax.fori_loop(0, blocks, step, jnp.zeros((SUB, lanes), jnp.int32))
    for side in range(2):
        acc[2 * plan.half + side, pl.ds(0, SUB), :] = live_total.astype(jnp.float32)
    outs = []
    for side, target in ((1, send), (0, keep)):
        outs.append(pltpu.make_async_copy(
            acc.at[pl.ds(side * plan.half, plan.half)],
            target.at[pl.ds(0, plan.half)], out_sem.at[2 * side]))
        outs.append(pltpu.make_async_copy(
            acc.at[2 * plan.half + side, pl.ds(0, SUB), :],
            target.at[plan.half, pl.ds(0, SUB), :], out_sem.at[2 * side + 1]))
    for copy in outs:
        copy.start()
    sum_rows = plan.cap * SUB
    tally_rows = round_up(plan.cap, PACK)
    for o in range(plan.shards):
        pay[o, plan.sum_at : plan.sum_at + sum_rows, :] = sums[
            o * sum_rows : (o + 1) * sum_rows, :
        ].astype(jnp.int16)
        pay[o, plan.count_at : plan.pay_rows, :] = tallies[
            o * tally_rows : (o + 1) * tally_rows, :
        ].astype(jnp.int16)
    copy = pltpu.make_async_copy(pay, pay_out, out_sem.at[4])
    copy.start()
    outs.append(copy)
    for copy in outs:
        copy.wait()


def ingest(plan, samples, counts, buckets, series, omap):
    blocks, rows, lanes = samples.shape
    half = jax.ShapeDtypeStruct((plan.half + 1, BINS, lanes), jnp.float32)
    pay = jax.ShapeDtypeStruct((plan.shards, plan.pay_rows, lanes), jnp.int16)
    return pl.pallas_call(
        functools.partial(ingest_kernel, plan),
        out_shape=(half, half, pay),
        in_specs=[SMEM, SMEM, SMEM, VMEM, ANY],
        out_specs=(ANY, ANY, ANY),
        scratch_shapes=[
            pltpu.VMEM((blocks, rows, lanes), jnp.bfloat16),
            pltpu.VMEM((2 * plan.half + 2, BINS, lanes), jnp.float32),
            pltpu.VMEM((plan.shards, plan.pay_rows, lanes), jnp.int16),
            pltpu.VMEM((plan.shards * plan.cap * SUB, lanes), jnp.int32),
            pltpu.VMEM((plan.shards * round_up(plan.cap, PACK), lanes), jnp.int32),
            pltpu.SMEM((plan.shards,), jnp.int32),
            pltpu.SemaphoreType.DMA((blocks,)),
            pltpu.SemaphoreType.DMA((5,)),
        ],
        compiler_params=pltpu.CompilerParams(vmem_limit_bytes=VMEM_LIMIT),
        name="ingest",
    )(counts, series, omap, buckets, samples)


def decode_live(tile):
    low = tile[:SUB].astype(jnp.float32)
    return low + tile[SUB:].astype(jnp.float32) * float(LIVE_BASE)


def exchange_kernel(plan, step, *refs):
    arrays = step + 2
    last = step == plan.bits
    ins, refs = refs[:arrays], refs[arrays:]
    outs, refs = refs[: 2 if last else 1], refs[2 if last else 1 :]
    f32buf, i16buf, f32tail, i16tail, stage, powers, sem, tail_sem, out_sem = refs
    lanes = f32buf.shape[-1]
    mine = (lax.axis_index("replica") >> 1) * plan.shards + lax.axis_index("shard")
    ways = plan.count(step) if not last else plan.ser_dev
    ser_dev = plan.ser_dev
    copies = []
    for g in range(ways // ser_dev):
        base = 0
        for i, bit in enumerate(plan.order[: step + 1]):
            base = base | ((mine ^ (1 << bit if i == step else 0)) & (1 << bit))
        j = base + plan.spread(g, step + 1) if not last else mine
        group = []
        for a in range(arrays):
            if a < 2:
                src = ins[a].at[pl.ds(j * ser_dev, ser_dev)]
                dst = f32buf.at[a, pl.ds(g * ser_dev, ser_dev)]
            else:
                start = pl.multiple_of(plan.squeeze(j, a - 1) * ser_dev * BINS, BINS)
                src = ins[a].at[pl.ds(start, ser_dev * BINS)]
                dst = i16buf.at[a - 2, pl.ds(g * ser_dev * BINS, ser_dev * BINS)]
            group.append((a, pltpu.make_async_copy(src, dst, sem.at[g * arrays + a]), j))
        copies.append(group)
    tails = []
    for a in range(arrays):
        if a < 2:
            src, dst = ins[a].at[plan.half, pl.ds(0, SUB), :], f32tail.at[a]
        else:
            n = plan.count(a - 2)
            size = round_up(n, PACK) + PACK
            src = ins[a].at[pl.ds(n * BINS, size)]
            dst = i16tail.at[a - 2, pl.ds(0, size)]
        tails.append(pltpu.make_async_copy(src, dst, tail_sem.at[a]))
    for copy in tails:
        copy.start()
    for group in copies:
        for _, copy, _ in group:
            copy.start()
    for copy in tails:
        copy.wait()
    live = f32tail[0] + f32tail[1]
    for a in range(2, arrays):
        n = round_up(plan.count(a - 2), PACK)
        live = live + decode_live(i16tail[a - 2, n : n + PACK, :])
        wide = i16tail[a - 2, :n, :].astype(jnp.float32)
        powers[a - 1, :n, :] = jnp.exp2(wide * (1.0 / 64)) * (1.0 / STEPS16)
    written = []
    for g, group in enumerate(copies):
        for _, copy, _ in group:
            copy.wait()
        for d in range(ser_dev):
            at = g * ser_dev + d
            value = f32buf[0, at] + f32buf[1, at]
            for a in range(2, arrays):
                source = plan.squeeze(group[a][2], a - 1) * ser_dev + d
                power = powers[a - 1, pl.ds(source, 1), :]
                coded = i16buf[a - 2, at * BINS : (at + 1) * BINS, :]
                value = value + coded.astype(jnp.float32) * power
            if last:
                outs[0][d] = value
            else:
                top = jnp.max(jnp.abs(value), axis=0, keepdims=True)
                top = jnp.maximum(top, 2.0**-126)
                power = jnp.floor(jnp.log2(top) * 64.0) + 2.0
                powers[0, pl.ds(at, 1), :] = power
                value = value * jnp.exp2(power * (-1.0 / 64)) * STEPS16
                stage[at * BINS : (at + 1) * BINS, :] = to_int16(
                    jnp.clip(value, -STEPS16, STEPS16)
                )
        if not last:
            region = pl.ds(g * ser_dev * BINS, ser_dev * BINS)
            copy = pltpu.make_async_copy(stage.at[region], outs[0].at[region], out_sem.at[g])
            copy.start()
            written.append(copy)
    if last:
        row = lax.broadcasted_iota(jnp.int32, (SUB, lanes), 0)
        place = row * lanes + lax.broadcasted_iota(jnp.int32, (SUB, lanes), 1)
        p = lax.axis_index("shard") * plan.ser_own + lax.axis_index("replica") * ser_dev
        for d in range(ser_dev):
            outs[1][d] = jnp.sum(jnp.where(place == p + d, live, 0.0))
        return
    n = round_up(ways, PACK)
    stage[ways * BINS : ways * BINS + n, :] = powers[0, :n, :].astype(jnp.int32).astype(jnp.int16)
    whole = live.astype(jnp.int32)
    high = whole // LIVE_BASE
    pair = jnp.concatenate([whole - high * LIVE_BASE, high], axis=0)
    stage[ways * BINS + n : ways * BINS + n + PACK, :] = pair.astype(jnp.int16)
    region = pl.ds(ways * BINS, n + PACK)
    copy = pltpu.make_async_copy(stage.at[region], outs[0].at[region], out_sem.at[len(copies)])
    copy.start()
    written.append(copy)
    for copy in written:
        copy.wait()


def exchange(plan, step, arrays, lanes):
    last = step == plan.bits
    ways = plan.ser_dev if last else plan.count(step)
    groups = ways // plan.ser_dev
    coded = max(1, step)
    tail = round_up(plan.count(0), PACK) + PACK
    if last:
        out_shape = (
            jax.ShapeDtypeStruct((plan.ser_dev, BINS, lanes), jnp.float32),
            jax.ShapeDtypeStruct((plan.ser_dev,), jnp.float32),
        )
        out_specs = (VMEM, SMEM)
        stage = PACK
    else:
        stage = plan.rows(step)
        out_shape = jax.ShapeDtypeStruct((stage, lanes), jnp.int16)
        out_specs = ANY
    return pl.pallas_call(
        functools.partial(exchange_kernel, plan, step),
        out_shape=out_shape,
        in_specs=[ANY] * (step + 2),
        out_specs=out_specs,
        scratch_shapes=[
            pltpu.VMEM((2, ways, BINS, lanes), jnp.float32),
            pltpu.VMEM((coded, ways * BINS, lanes), jnp.int16),
            pltpu.VMEM((2, SUB, lanes), jnp.float32),
            pltpu.VMEM((coded, tail, lanes), jnp.int16),
            pltpu.VMEM((stage, lanes), jnp.int16),
            pltpu.VMEM((coded + 1, round_up(plan.count(0), PACK), lanes), jnp.float32),
            pltpu.SemaphoreType.DMA((groups * (step + 2),)),
            pltpu.SemaphoreType.DMA((step + 2,)),
            pltpu.SemaphoreType.DMA((groups + 1,)),
        ],
        compiler_params=pltpu.CompilerParams(vmem_limit_bytes=VMEM_LIMIT),
        name=f"exchange{step}",
    )(*arrays)


def cold_kernel(plan, pay, out):
    lanes = out.shape[-1]
    row = lax.broadcasted_iota(jnp.int32, (SUB, lanes), 0)
    tally = pay[0, plan.count_at : plan.pay_rows, :].astype(jnp.int32)
    for c in range(plan.cap):
        count = jnp.broadcast_to(tally[c : c + 1, :], (SUB, lanes))
        n = jnp.clip(count - MINUTE * row, 0, MINUTE).astype(jnp.float32)
        filled = n > 0
        ends = pay[0, c * 2 * SUB : (c + 1) * 2 * SUB, :].astype(jnp.float32) * (LIMIT / STEPS16)
        mean = pay[0, plan.sum_at + c * SUB : plan.sum_at + (c + 1) * SUB, :].astype(jnp.float32)
        out[c, 0] = jnp.where(filled, ends[:SUB], 0.0)
        out[c, 1] = jnp.where(filled, ends[SUB:], 0.0)
        out[c, 2] = mean * (LIMIT / STEPS16) * n
        out[c, 3] = n


def cold(plan, pay, minutes):
    shards, rows, lanes = pay.shape
    return pl.pallas_call(
        functools.partial(cold_kernel, plan),
        out_shape=jax.ShapeDtypeStruct((shards * plan.cap, 4, minutes, lanes), jnp.float32),
        grid=(shards,),
        in_specs=[pl.BlockSpec((1, rows, lanes), lambda i: (i, 0, 0))],
        out_specs=pl.BlockSpec((plan.cap, 4, minutes, lanes), lambda i: (i, 0, 0, 0)),
        compiler_params=pltpu.CompilerParams(dimension_semantics=("arbitrary",)),
        name="cold",
    )(pay)


def body(samples, counts, buckets, series, omap):
    blocks, rows, lanes = samples.shape
    plan = Plan(lax.axis_size("shard"), lax.axis_size("replica"), omap.shape[0], blocks)
    send, keep, pay = ingest(plan, samples, counts, buckets, series, omap)
    arrays = [keep, lax.ppermute(send, *plan.partner(-1))]
    pay = lax.all_to_all(pay, "shard", split_axis=0, concat_axis=0, tiled=True)
    for step in range(plan.bits):
        coded = exchange(plan, step, arrays, lanes)
        arrays.append(lax.ppermute(coded, *plan.partner(step)))
    sketches, live_rows = exchange(plan, plan.bits, arrays, lanes)
    stats = cold(plan, pay, rows // MINUTE)
    return stats.reshape((1, 1) + stats.shape), sketches, live_rows


def solution(mesh):
    both = ("shard", "replica")
    return jax.shard_map(
        body,
        mesh=mesh,
        in_specs=(P(both, None, None), P(both), P(both, None), P(both), P()),
        out_specs=(
            P("shard", "replica", None, None, None, None),
            P(both, None, None),
            P(both),
        ),
        check_vma=False,
    )
```

time: 318 us -> 81.7 us (0.26)
  waiting for transfers between devices: 188 us -> 22.9 us
  Pallas kernels: 0 us -> 37.8 us
  matrix products: 32.9 us -> 0 us
  other arithmetic: 25.6 us -> 0 us
  local copies, waits for them, and re-layouts: 26.5 us -> 5.03 us
  between operations: 14.2 us -> 0.69 us
  starting transfers between devices: 23 us -> 14.7 us
  blocking collectives: 6.8 us -> 0 us
    all_to_all x4 -> x1, waiting for transfers between devices: 186 us -> 0.01 us  [body(): pay = lax.all_to_all(pay, 'shard', split_axis=0, concat_axis=0, tiled=True)]
    pallas_call x0 -> x7, Pallas kernels: none -> 37.8 us  [the longest x1 21.2 us: ingest(): pl.pallas_call(functools.partial(ingest_kernel, plan), out_shape=(half, h...]
    dot_general x3 -> x0, matrix products: 32.9 us -> none  [the longest x1 18.5 us: bucket_sketch(): jnp.einsum('nks,nsl->nkl', table, values, preferred_element_type=jnp.floa...]
    ppermute x0 -> x5, waiting for transfers between devices: none -> 22.9 us  [the longest x4 22.9 us: body(): arrays.append(lax.ppermute(coded, *plan.partner(step)))]
    all_to_all x4 -> x1, starting transfers between devices: 22.9 us -> 6.81 us  [body(): pay = lax.all_to_all(pay, 'shard', split_axis=0, concat_axis=0, tiled=True)]
    select_n x6 -> x0, other arithmetic: 14.9 us -> none  [the longest x1 12.3 us: body(): sketch_buf = jnp.where(used[:, None, None], sketch_all[source], 0.0)]
    gather x5 -> x0, local copies, waits for them, and re-layouts: 10.9 us -> none  [the longest x1 6.49 us: body(): sketch_buf = jnp.where(used[:, None, None], sketch_all[source], 0.0)]
    reduce_min x1 -> x0, other arithmetic: 8.5 us -> none  [minute_stats(): lowest = jnp.min(jnp.where(live, data, jnp.inf), axis=2)]
  transfers between devices with their start and end apart: 5 -> 6, of which waited for: 3 -> 3; matrix products, arithmetic and copies ran while one was open for 25% -> 0% of each run, Pallas kernels for 0% -> 18%
where the time goes in v1:
time: 81.7 us; the launch traced here: 81.1 us
  Pallas kernels  37.8 us (46%)
  waiting for transfers between devices  22.9 us (28%)
  starting transfers between devices  14.7 us (18%)
  local copies, waits for them, and re-layouts  5.03 us (6%)
    ppermute x4, waiting for transfers between devices, body(): arrays.append(lax.ppermute(coded, *plan.partner(step)))  22.9 us
    pallas_call x1, Pallas kernels, ingest(): pl.pallas_call(functools.partial(ingest_kernel, plan), out_shape=(half, h...  21.2 us
    pallas_call x5, Pallas kernels, exchange(): pl.pallas_call(functools.partial(exchange_kernel, plan, step), out_shape=...  11.2 us
    ppermute x4, starting transfers between devices, body(): arrays.append(lax.ppermute(coded, *plan.partner(step)))  7.34 us
    all_to_all x1, starting transfers between devices, body(): pay = lax.all_to_all(pay, 'shard', split_axis=0, concat_axis=0, tiled=True)  6.81 us
    pallas_call x1, Pallas kernels, cold(): pl.pallas_call(functools.partial(cold_kernel, plan), out_shape=jax.ShapeD...  5.42 us
    unnamed x12, local copies, waits for them, and re-layouts  5.03 us
  transfers between devices with their start and end apart: 6, of which 3 were waited for; matrix products, arithmetic and copies ran while one was open for 0% of the time, Pallas kernels for 18%

profile of v1, /device:TPU:0, one launch (start us, length us, event | category | flops | bytes accessed | tf_op | source)
XLA Modules:
  0.0 81.1 jit_solution(1475282364868611528)
XLA Ops:
  0.6 21.2 %ingest.1 = (f32[33,128,128]{2,1,0:T(8,128)}, f32[33,128,128]{2,1,0:T(8,128)}, s16[8,400,128]{2,1,0:T(8,128)(2,1)}) custom-call(s32[64]{0:T(128)} %counts.1, s32[64]{0:T(128)} %series.1, s32[64]{0:T(128)} %omap.1, s32[64,480]{1,0:T(8,128)} %buckets.1, bf16[64,480,128]{2,1,0:T(8,128)(2,1)} %samples.1), custom_call_target="tpu_custom_call" | custom-call | tf_op jit(solution)/shard_map/ingest/pallas_call | solution.py:232
  21.8 0.6 collective-permute-start
  22.4 6.8 %all-to-all-start = ((s16[8,400,128]{2,1,0:T(8,128)(2,1)}), s16[8,400,128]{2,1,0:T(8,128)(2,1)S(1)}, u32[]{:S(2)}, u32[]{:S(2)}) async-start(s16[8,400,128]{2,1,0:T(8,128)(2,1)} %get-tuple-element.8), calls=%async_computation | async-start | bytes 1638400 | tf_op jit(solution)/shard_map/all_to_all | solution.py:428
  29.2 0.0 collective-permute-done.refs_1_
  29.2 0.0 copy-start
  29.2 1.3 %copy-done = f32[33,128,128]{2,1,0:T(8,128)} copy-done((f32[33,128,128]{2,1,0:T(8,128)}, f32[33,128,128]{2,1,0:T(8,128)S(1)}, u32[]{:S(2)}) %copy-start) | copy-done | bytes 2162712
  30.5 2.9 %exchange0.1 = s16[2080,128]{1,0:T(8,128)(2,1)} custom-call(f32[33,128,128]{2,1,0:T(8,128)} %get-tuple-element.9.refs_0_, f32[33,128,128]{2,1,0:T(8,128)} %copy-done), custom_call_target="tpu_custom_call" | custom-call | tf_op jit(solution)/shard_map/exchange0/pallas_call | solution.py:373
  33.4 1.6 %collective-permute-start.1 = (s16[2080,128]{1,0:T(8,128)(2,1)}, s16[2080,128]{1,0:T(8,128)(2,1)S(1)}, u32[]{:S(2)}, u32[]{:S(2)}) collective-permute-start(s16[2080,128]{1,0:T(8,128)(2,1)} %exchange0.1), channel_id=1, source_target_pairs={{0,2},{1,3},{2,0},{3,1},{4,6},{5,7},{6,4},{7,5},{8,10},{9,11},{10,... | collective-permute-start | bytes 1597448 | tf_op jit(solution)/shard_map/ppermute | solution.py:431
  35.0 12.9 %collective-permute-done.1.refs_2_ = s16[2080,128]{1,0:T(8,128)(2,1)S(1)} collective-permute-done((s16[2080,128]{1,0:T(8,128)(2,1)}, s16[2080,128]{1,0:T(8,128)(2,1)S(1)}, u32[]{:S(2)}, u32[]{:S(2)}) %collective-permute-start.1) | collective-permute-done | bytes 532512 | tf_op jit(solution)/shard_map/ppermute | solution.py:431
  47.9 0.0 copy-start.1
  47.9 0.8 %copy-done.1 = s16[2080,128]{1,0:T(8,128)(2,1)} copy-done((s16[2080,128]{1,0:T(8,128)(2,1)}, s16[2080,128]{1,0:T(8,128)(2,1)S(1)}, u32[]{:S(2)}) %copy-start.1) | copy-done | bytes 532504
  48.7 2.4 %exchange1.1 = s16[1056,128]{1,0:T(8,128)(2,1)} custom-call(f32[33,128,128]{2,1,0:T(8,128)} %get-tuple-element.9.refs_0_, f32[33,128,128]{2,1,0:T(8,128)} %copy-done, s16[2080,128]{1,0:T(8,128)(2,1)} %copy-done.1), custom_call_target="tpu_custom_call" | custom-call | tf_op jit(solution)/shard_map/exchange1/pallas_call | solution.py:373
  51.1 1.8 %collective-permute-start.2 = (s16[1056,128]{1,0:T(8,128)(2,1)}, s16[1056,128]{1,0:T(8,128)(2,1)S(1)}, u32[]{:S(2)}, u32[]{:S(2)}) collective-permute-start(s16[1056,128]{1,0:T(8,128)(2,1)} %exchange1.1), channel_id=1, source_target_pairs={{0,4},{4,0},{8,12},{12,8},{16,20},{20,16},{24,28},{28,24},{1,5},{5... | collective-permute-start | bytes 811016 | tf_op jit(solution)/shard_map/ppermute | solution.py:431
  52.9 6.2 %collective-permute-done.2.refs_3_ = s16[1056,128]{1,0:T(8,128)(2,1)S(1)} collective-permute-done((s16[1056,128]{1,0:T(8,128)(2,1)}, s16[1056,128]{1,0:T(8,128)(2,1)S(1)}, u32[]{:S(2)}, u32[]{:S(2)}) %collective-permute-start.2) | collective-permute-done | bytes 270368 | tf_op jit(solution)/shard_map/ppermute | solution.py:431
  59.1 0.0 copy-start.3
  59.1 0.7 copy-done.3
  59.8 2.0 %exchange2.1 = s16[544,128]{1,0:T(8,128)(2,1)} custom-call(f32[33,128,128]{2,1,0:T(8,128)} %get-tuple-element.9.refs_0_, f32[33,128,128]{2,1,0:T(8,128)} %copy-done, s16[2080,128]{1,0:T(8,128)(2,1)} %copy-done.1, s16[1056,128]{1,0:T(8,128)(2,1)} %copy-done.3), custom_call_target="tpu_custom_call" | custom-call | tf_op jit(solution)/shard_map/exchange2/pallas_call | solution.py:373
  61.8 1.5 %collective-permute-start.3 = (s16[544,128]{1,0:T(8,128)(2,1)}, s16[544,128]{1,0:T(8,128)(2,1)S(1)}, u32[]{:S(2)}, u32[]{:S(2)}) collective-permute-start(s16[544,128]{1,0:T(8,128)(2,1)} %exchange2.1), channel_id=1, source_target_pairs={{0,8},{4,12},{8,0},{12,4},{16,24},{20,28},{24,16},{28,20},{1,9},{5... | collective-permute-start | bytes 417800 | tf_op jit(solution)/shard_map/ppermute | solution.py:431
  63.4 3.8 %collective-permute-done.3.refs_4_ = s16[544,128]{1,0:T(8,128)(2,1)S(1)} collective-permute-done((s16[544,128]{1,0:T(8,128)(2,1)}, s16[544,128]{1,0:T(8,128)(2,1)S(1)}, u32[]{:S(2)}, u32[]{:S(2)}) %collective-permute-start.3) | collective-permute-done | bytes 139296 | tf_op jit(solution)/shard_map/ppermute | solution.py:431
  67.2 0.0 copy-start.4
  67.2 0.7 copy-done.4
  67.8 1.9 %exchange3.1 = s16[288,128]{1,0:T(8,128)(2,1)} custom-call(f32[33,128,128]{2,1,0:T(8,128)} %get-tuple-element.9.refs_0_, f32[33,128,128]{2,1,0:T(8,128)} %copy-done, s16[2080,128]{1,0:T(8,128)(2,1)} %copy-done.1, s16[1056,128]{1,0:T(8,128)(2,1)} %copy-done.3, s16[544,128]{1,0:T(8,128)(2,1)} %copy-done.4), custom_call_target="tpu_custom_call" | custom-call | tf_op jit(solution)/shard_map/exchange3/pallas_call | solution.py:373
  69.8 2.4 %collective-permute-start.4 = (s16[288,128]{1,0:T(8,128)(2,1)}, s16[288,128]{1,0:T(8,128)(2,1)S(1)}, u32[]{:S(2)}, u32[]{:S(2)}) collective-permute-start(s16[288,128]{1,0:T(8,128)(2,1)} %exchange3.1), channel_id=1, source_target_pairs={{0,16},{4,20},{8,24},{12,28},{16,0},{20,4},{24,8},{28,12},{1,17},{... | collective-permute-start | bytes 221192 | tf_op jit(solution)/shard_map/ppermute | solution.py:431
  72.2 0.0 all-to-all-done.pay
  72.2 0.0 copy-start.2
  72.2 0.9 %copy-done.2 = s16[8,400,128]{2,1,0:T(8,128)(2,1)} copy-done((s16[8,400,128]{2,1,0:T(8,128)(2,1)}, s16[8,400,128]{2,1,0:T(8,128)(2,1)S(1)}, u32[]{:S(2)}) %copy-start.2) | copy-done | bytes 819224
  73.1 5.4 %cold.1 = f32[128,4,8,128]{3,2,1,0:T(8,128)} custom-call(s16[8,400,128]{2,1,0:T(8,128)(2,1)} %copy-done.2), custom_call_target="tpu_custom_call" | custom-call | tf_op jit(solution)/shard_map/cold/pallas_call | solution.py:412
  78.5 0.0 collective-permute-done.4.refs_5_
  78.5 0.0 copy-start.5
  78.5 0.6 copy-done.5
  79.1 2.0 %exchange4.1 = (f32[2,128,128]{2,1,0:T(8,128)}, f32[2]{0:T(128)}) custom-call(f32[33,128,128]{2,1,0:T(8,128)} %get-tuple-element.9.refs_0_, f32[33,128,128]{2,1,0:T(8,128)} %copy-done, s16[2080,128]{1,0:T(8,128)(2,1)} %copy-done.1, s16[1056,128]{1,0:T(8,128)(2,1)} %copy-done.3, s16[544,128]{1,0:T(8,128)(2,1)} %copy-done.4, s16[288,128]{1,0:T(8,128)(2,1)} %copy-done.5), custom_call_target="tpu_custom_call" | custom-call | tf_op jit(solution)/shard_map/exchange4/pallas_call | solution.py:373
Async XLA Ops:
  21.8 7.4 %collective-permute-start = (f32[33,128,128]{2,1,0:T(8,128)}, f32[33,128,128]{2,1,0:T(8,128)S(1)}, u32[]{:S(2)}, u32[]{:S(2)}) collective-permute-start(f32[33,128,128]{2,1,0:T(8,128)} %get-tuple-element.10), channel_id=1, source_target_pairs={{0,1},{1,0},{2,3},{3,2},{4,5},{5,4},{6,7},{7,6},{8,9},{9,8},{10,11... | collective-permute-start | bytes 6488072 | tf_op jit(solution)/shard_map/ppermute | solution.py:427
  22.4 49.9 %all-to-all-start = ((s16[8,400,128]{2,1,0:T(8,128)(2,1)}), s16[8,400,128]{2,1,0:T(8,128)(2,1)S(1)}, u32[]{:S(2)}, u32[]{:S(2)}) async-start(s16[8,400,128]{2,1,0:T(8,128)(2,1)} %get-tuple-element.8), calls=%async_computation | async-start | bytes 1638400 | tf_op jit(solution)/shard_map/all_to_all | solution.py:428
  29.2 1.3 %copy-start = (f32[33,128,128]{2,1,0:T(8,128)}, f32[33,128,128]{2,1,0:T(8,128)S(1)}, u32[]{:S(2)}) copy-start(f32[33,128,128]{2,1,0:T(8,128)S(1)} %collective-permute-done.refs_1_) | copy-start | bytes 6488068
  33.4 14.5 %collective-permute-start.1 = (s16[2080,128]{1,0:T(8,128)(2,1)}, s16[2080,128]{1,0:T(8,128)(2,1)S(1)}, u32[]{:S(2)}, u32[]{:S(2)}) collective-permute-start(s16[2080,128]{1,0:T(8,128)(2,1)} %exchange0.1), channel_id=1, source_target_pairs={{0,2},{1,3},{2,0},{3,1},{4,6},{5,7},{6,4},{7,5},{8,10},{9,11},{10,... | collective-permute-start | bytes 1597448 | tf_op jit(solution)/shard_map/ppermute | solution.py:431
  47.9 0.8 %copy-start.1 = (s16[2080,128]{1,0:T(8,128)(2,1)}, s16[2080,128]{1,0:T(8,128)(2,1)S(1)}, u32[]{:S(2)}) copy-start(s16[2080,128]{1,0:T(8,128)(2,1)S(1)} %collective-permute-done.1.refs_2_) | copy-start | bytes 1597444
  51.1 8.0 %collective-permute-start.2 = (s16[1056,128]{1,0:T(8,128)(2,1)}, s16[1056,128]{1,0:T(8,128)(2,1)S(1)}, u32[]{:S(2)}, u32[]{:S(2)}) collective-permute-start(s16[1056,128]{1,0:T(8,128)(2,1)} %exchange1.1), channel_id=1, source_target_pairs={{0,4},{4,0},{8,12},{12,8},{16,20},{20,16},{24,28},{28,24},{1,5},{5... | collective-permute-start | bytes 811016 | tf_op jit(solution)/shard_map/ppermute | solution.py:431
  59.1 0.7 copy-start.3
  61.8 5.3 %collective-permute-start.3 = (s16[544,128]{1,0:T(8,128)(2,1)}, s16[544,128]{1,0:T(8,128)(2,1)S(1)}, u32[]{:S(2)}, u32[]{:S(2)}) collective-permute-start(s16[544,128]{1,0:T(8,128)(2,1)} %exchange2.1), channel_id=1, source_target_pairs={{0,8},{4,12},{8,0},{12,4},{16,24},{20,28},{24,16},{28,20},{1,9},{5... | collective-permute-start | bytes 417800 | tf_op jit(solution)/shard_map/ppermute | solution.py:431
  67.2 0.7 copy-start.4
  69.8 8.7 %collective-permute-start.4 = (s16[288,128]{1,0:T(8,128)(2,1)}, s16[288,128]{1,0:T(8,128)(2,1)S(1)}, u32[]{:S(2)}, u32[]{:S(2)}) collective-permute-start(s16[288,128]{1,0:T(8,128)(2,1)} %exchange3.1), channel_id=1, source_target_pairs={{0,16},{4,20},{8,24},{12,28},{16,0},{20,4},{24,8},{28,12},{1,17},{... | collective-permute-start | bytes 221192 | tf_op jit(solution)/shard_map/ppermute | solution.py:431
  72.2 0.9 %copy-start.2 = (s16[8,400,128]{2,1,0:T(8,128)(2,1)}, s16[8,400,128]{2,1,0:T(8,128)(2,1)S(1)}, u32[]{:S(2)}) copy-start(s16[8,400,128]{2,1,0:T(8,128)(2,1)S(1)} %all-to-all-done.pay) | copy-start | bytes 2457604
  78.5 0.6 copy-start.5

commit v2 on v0

v2 whole, which is shorter than its diff:
```python
import functools

import jax
import jax.numpy as jnp
from jax import lax
from jax.experimental import pallas as pl
from jax.experimental.pallas import tpu as pltpu
from jax.sharding import PartitionSpec as P


BINS = 128
MINUTE = 60
SUB = 8
PACK = 16
LIMIT = 6.0
STEPS16 = 32767.0
LIVE_BASE = 16384
MIB = 2**20

ANY = pl.BlockSpec(memory_space=pl.ANY)
HBM = pl.BlockSpec(memory_space=pltpu.HBM)
SMEM = pl.BlockSpec(memory_space=pltpu.SMEM)
VMEM = pl.BlockSpec(memory_space=pltpu.VMEM)


def round_up(n, m):
    return -(-n // m) * m


def to_int16(x):
    return jnp.floor(x + 0.5).astype(jnp.int32).astype(jnp.int16)


def split(x, n):
    if n & (n - 1) == 0:
        return x >> (n.bit_length() - 1), x & (n - 1)
    return x // n, x - (x // n) * n


class Plan:
    def __init__(self, shards, replicas, series, blocks):
        self.shards, self.replicas, self.series = shards, replicas, series
        self.ser_own = series // shards
        self.ser_dev = self.ser_own // replicas
        self.cap = max(2, (2 * blocks + shards - 1) // shards)
        self.sbits = shards.bit_length() - 1
        self.groups = (replicas // 2) * shards
        self.bits = self.groups.bit_length() - 1
        assert 2**self.bits == self.groups and self.bits > self.sbits > 0 and self.ser_dev == 2
        order = list(range(self.sbits, self.bits)) + list(range(self.sbits))
        first, second = order[0], order[-self.sbits]
        rest = [bit for bit in order if bit not in (first, second)]
        self.orders = ([first, second] + rest, [second, first] + rest)
        self.sum_at = self.cap * 2 * SUB
        self.count_at = self.sum_at + round_up(self.cap * SUB, PACK)
        self.pay_rows = self.count_at + round_up(self.cap, PACK)

    def partner(self, bit):
        if bit < 0:
            axis, size, flip = "replica", self.replicas, 1
        elif bit >= self.sbits:
            axis, size, flip = "replica", self.replicas, 2 << (bit - self.sbits)
        else:
            axis, size, flip = "shard", self.shards, 1 << bit
        return axis, [(i, i ^ flip) for i in range(size)]

    def ways(self, step):
        return 1 << (self.bits - step - 1)

    def count(self, step):
        return self.ways(step) * (1 if step < 2 else 2)

    def rows(self, step):
        n = self.count(step)
        return n * BINS + round_up(n, PACK) + PACK

    def squeeze(self, j, color, steps):
        out, at = 0, 0
        for bit in range(self.bits):
            if bit not in self.orders[color][:steps]:
                out = out + (((j >> bit) & 1) << at)
                at += 1
        return out

    def spread(self, index, color, steps):
        out, at = 0, 0
        for bit in range(self.bits):
            if bit not in self.orders[color][:steps]:
                out = out | (((index >> at) & 1) << bit)
                at += 1
        return out

    def settled(self, mine, color, steps, flip):
        out = 0
        for i, bit in enumerate(self.orders[color][:steps]):
            out = out | ((mine ^ (1 << bit if flip and i == steps - 1 else 0)) & (1 << bit))
        return out

    def position(self, j, away, me, d):
        r = ((j >> self.sbits) << 1) | ((me & 1) ^ away)
        return (j & (self.shards - 1)) * self.ser_own + r * self.ser_dev + d


def reduce_rows(parts, op, row):
    out = list(parts)
    for width in (4, 2, 1):
        low = (row & width) == 0
        merged = []
        for i in range(width):
            a, b = out[i], out[i + width]
            first = jnp.where(low, a, b)
            other = jnp.where(low, b, a)
            up = pltpu.roll(other, SUB - width, 0)
            if width == 4:
                turned = up
            else:
                turned = jnp.where(low, up, pltpu.roll(other, width, 0))
            merged.append(op(first, turned))
        out = merged
    return out[0]


def sketch_kernel(
    plan, chunk, counts, series, omap, buckets, samples,
    send_far, keep_far, send_near, keep_near, marks, buf, total, sem, mark_sem,
):
    blocks, rows, lanes = buf.shape
    me = lax.axis_index("replica")
    mine = (me >> 1) * plan.shards + lax.axis_index("shard")
    fetch = pltpu.make_async_copy(buckets, marks, mark_sem)
    fetch.start()

    def copies(i):
        at = pl.ds(i * chunk, chunk)
        return pltpu.make_async_copy(samples.at[at], buf.at[at], sem.at[i])

    for i in range(blocks // chunk):
        copies(i).start()

    @pl.loop(0, plan.series)
    def _(i):
        total[i] = jnp.zeros((BINS, lanes), jnp.float32)

    sub = lax.broadcasted_iota(jnp.int32, (SUB, lanes), 0)
    place = sub * lanes + lax.broadcasted_iota(jnp.int32, (SUB, lanes), 1)
    when = lax.broadcasted_iota(jnp.int32, (1, rows), 1)
    levels = lax.broadcasted_iota(jnp.int32, (BINS, rows), 0)
    fetch.wait()

    def step(i, live):
        copies(i).wait()
        sums = []
        for u in range(chunk):
            b = i * chunk + u
            p = omap[series[b]]
            mark = jnp.where(when < counts[b], marks[pl.ds(b, 1), :], -1)
            hot = (jnp.broadcast_to(mark, (BINS, rows)) == levels).astype(jnp.float32)
            hot = hot.astype(jnp.bfloat16)
            sums.append((p, jnp.dot(hot, buf[b], preferred_element_type=jnp.float32)))
            live = live + jnp.where(place == p, counts[b], 0)
        for p, out in sums:
            total[p] += out
        return live

    live = lax.fori_loop(0, blocks // chunk, step, jnp.zeros((SUB, lanes), jnp.int32))
    top = plan.groups * BINS
    for ref in (send_far, keep_far):
        ref[top : top + SUB, :] = live.astype(jnp.float32)
    ways = plan.ways(0)
    for far, away, ref in (
        (1, 1, send_far), (1, 0, keep_far), (0, 1, send_near), (0, 0, keep_near),
    ):
        for color in range(2):
            fixed = plan.settled(mine, color, 1, far)

            @pl.loop(0, ways, unroll=4)
            def _(i):
                j = fixed | plan.spread(i, color, 1)
                at = pl.ds(pl.multiple_of((color * ways + i) * BINS, BINS), BINS)
                ref[at, :] = total[plan.position(j, away, me, color)]


def sketch(plan, samples, counts, buckets, series, omap):
    blocks, rows, lanes = samples.shape
    chunk = 8
    far = jax.ShapeDtypeStruct((plan.groups * BINS + SUB, lanes), jnp.float32)
    near = jax.ShapeDtypeStruct((plan.groups * BINS, lanes), jnp.float32)
    return pl.pallas_call(
        functools.partial(sketch_kernel, plan, chunk),
        out_shape=(far, far, near, near),
        in_specs=[SMEM, SMEM, SMEM, HBM, HBM],
        out_specs=(VMEM,) * 4,
        scratch_shapes=[
            pltpu.VMEM((blocks, rows), jnp.int32),
            pltpu.VMEM((blocks, rows, lanes), jnp.bfloat16),
            pltpu.VMEM((plan.series, BINS, lanes), jnp.float32),
            pltpu.SemaphoreType.DMA((blocks // chunk,)),
            pltpu.SemaphoreType.DMA,
        ],
        compiler_params=pltpu.CompilerParams(vmem_limit_bytes=57 * MIB),
        name="sketch",
    )(counts, series, omap, buckets, samples)


def minute_ends(x, minutes, op, worst, row16):
    fill = jnp.full((PACK, x.shape[1]), worst, x.dtype)
    out = []
    for m in range(minutes):
        lo, hi = m * MINUTE, (m + 1) * MINUTE
        total = None
        for v in range(lo // PACK, -(-hi // PACK)):
            tile = x[v * PACK : (v + 1) * PACK]
            if v * PACK < lo:
                tile = jnp.where(row16 >= lo - v * PACK, tile, fill)
            if (v + 1) * PACK > hi:
                tile = jnp.where(row16 < hi - v * PACK, tile, fill)
            total = tile if total is None else op(total, tile)
        wide = total.astype(jnp.float32)
        out.append(op(wide[:SUB], wide[SUB:]))
    return out


def part_ends(x, live, op, worst):
    x = jnp.where(live, x, jnp.full(x.shape, worst, x.dtype))
    total = x[:PACK]
    for v in range(1, x.shape[0] // PACK):
        total = op(total, x[v * PACK : (v + 1) * PACK])
    wide = total.astype(jnp.float32)
    out = op(wide[:SUB], wide[SUB:])
    for width in (4, 2, 1):
        out = op(out, pltpu.roll(out, width, 0))
    return out


def stats_kernel(
    plan, counts, series, omap, samples, after, pay, buf, sums, tallies, used, sem
):
    blocks, rows, lanes = buf.shape
    minutes = rows // MINUTE
    copies = lambda b: pltpu.make_async_copy(samples.at[b], buf.at[b], sem.at[b])

    @pl.loop(0, blocks)
    def _(b):
        copies(b).start()

    for o in range(plan.shards):
        used[o] = 0
    tallies[...] = jnp.zeros_like(tallies)
    when = lax.broadcasted_iota(jnp.int32, (1, rows), 1)
    which = when // MINUTE
    levels = lax.broadcasted_iota(jnp.int32, (PACK, rows), 0)
    sub = lax.broadcasted_iota(jnp.int32, (SUB, lanes), 0)
    row16 = lax.broadcasted_iota(jnp.int32, (PACK, lanes), 0)
    window = round_up(MINUTE + PACK - 4, PACK)
    near = lax.broadcasted_iota(jnp.int32, (window, lanes), 0)
    scale = STEPS16 / LIMIT

    def step(b, _):
        count = counts[b]
        o, _ = split(omap[series[b]], plan.ser_own)
        c = used[o]
        used[o] = c + 1
        copies(b).wait()
        x = buf[b]
        whole = jnp.broadcast_to(jnp.where(when < count, which, -1), (PACK, rows))
        ones = (whole == levels).astype(jnp.float32).astype(jnp.bfloat16)
        total = jnp.dot(ones, x, preferred_element_type=jnp.float32)[:SUB]
        part = count // MINUTE
        start = jnp.minimum((part * MINUTE) // PACK, (rows - window) // PACK) * PACK
        start = pl.multiple_of(start, PACK)
        some = buf[b, pl.ds(start, window), :]
        live = (near >= part * MINUTE - start) & (near < count - start)
        ends = []
        for op, worst in ((jnp.minimum, jnp.inf), (jnp.maximum, -jnp.inf)):
            end = reduce_rows(minute_ends(x, minutes, op, worst, row16), op, sub)
            ends.append(jnp.where(sub == part, part_ends(some, live, op, worst), end))
        n = jnp.clip(count - MINUTE * sub, 0, MINUTE).astype(jnp.float32)
        filled = n > 0
        ends = [jnp.where(filled, end, 0.0) * scale for end in ends]
        at = pl.ds(pl.multiple_of(c * 2 * SUB, 2 * SUB), 2 * SUB)
        pay[o, at, :] = to_int16(jnp.concatenate(ends, axis=0))
        mean = jnp.clip(total / jnp.maximum(n, 1.0), -LIMIT, LIMIT) * scale
        at = pl.ds(pl.multiple_of((o * plan.cap + c) * SUB, SUB), SUB)
        sums[at, :] = jnp.floor(mean + 0.5).astype(jnp.int32)
        at = pl.ds(o * round_up(plan.cap, PACK) + c, 1)
        tallies[at, :] = jnp.full((1, lanes), count, jnp.int32)
        return 0

    lax.fori_loop(0, blocks, step, 0)
    sum_rows = plan.cap * SUB
    tally_rows = round_up(plan.cap, PACK)
    for o in range(plan.shards):
        pay[o, plan.sum_at : plan.sum_at + sum_rows, :] = sums[
            o * sum_rows : (o + 1) * sum_rows, :
        ].astype(jnp.int16)
        pay[o, plan.count_at : plan.pay_rows, :] = tallies[
            o * tally_rows : (o + 1) * tally_rows, :
        ].astype(jnp.int16)


def minute_stats(plan, samples, counts, series, omap, after):
    blocks, rows, lanes = samples.shape
    return pl.pallas_call(
        functools.partial(stats_kernel, plan),
        out_shape=jax.ShapeDtypeStruct((plan.shards, plan.pay_rows, lanes), jnp.int16),
        in_specs=[SMEM, SMEM, SMEM, HBM, VMEM],
        out_specs=VMEM,
        scratch_shapes=[
            pltpu.VMEM((blocks, rows, lanes), jnp.bfloat16),
            pltpu.VMEM((plan.shards * plan.cap * SUB, lanes), jnp.int32),
            pltpu.VMEM((plan.shards * round_up(plan.cap, PACK), lanes), jnp.int32),
            pltpu.SMEM((plan.shards,), jnp.int32),
            pltpu.SemaphoreType.DMA((blocks,)),
        ],
        compiler_params=pltpu.CompilerParams(vmem_limit_bytes=57 * MIB),
        name="minute_stats",
    )(counts, series, omap, samples, after)


def decode_live(tile):
    low = tile[:SUB].astype(jnp.float32)
    return low + tile[SUB:].astype(jnp.float32) * float(LIVE_BASE)


def exchange_kernel(plan, step, lanes, *refs):
    last = step == plan.bits
    arrays = min(step, 2) * 2 + max(step - 2, 0)
    parts, coded, refs = refs[:2], refs[2 : 2 + arrays], refs[2 + arrays :]
    if step:
        live, refs = refs[0][...], refs[1:]
    else:
        top = plan.groups * BINS
        live = parts[0][top : top + SUB, :] + parts[1][top : top + SUB, :]
    outs, powers = refs[:-1], refs[-1]
    me = lax.axis_index("replica")
    mine = (me >> 1) * plan.shards + lax.axis_index("shard")
    received = []
    for a, ref in enumerate(coded):
        at, color = (a // 2, a % 2) if a < 4 else (a - 2, None)
        n = plan.count(at)
        tail = round_up(n, PACK)
        if not color:
            live = live + decode_live(ref[n * BINS + tail : n * BINS + tail + PACK, :])
        wide = ref[n * BINS : n * BINS + tail, :].astype(jnp.float32)
        powers[a + 2, :tail, :] = jnp.exp2(wide * (1.0 / 64)) * (1.0 / STEPS16)
        received.append((at, color, ref))
    ways = 1 if last else plan.ways(step)
    if step == 0:
        outs[2][...] = live
    for color in range(2):
        fixed = plan.settled(mine, color, min(step + 1, plan.bits), not last)
        for g in range(ways):
            j = fixed if last else fixed | plan.spread(g, color, step + 1)
            first = color * plan.ways(0) + plan.squeeze(j, color, 1)
            rows = pl.ds(pl.multiple_of(first * BINS, BINS), BINS)
            value = parts[0][rows, :] + parts[1][rows, :]
            for a, (at, its, ref) in enumerate(received):
                if its is None or its == color:
                    source = plan.squeeze(j, color, at + 1)
                    source = source if its == color else source * 2 + color
                    rows = pl.ds(pl.multiple_of(source * BINS, BINS), BINS)
                    power = powers[a + 2, pl.ds(source, 1), :]
                    value = value + ref[rows, :].astype(jnp.float32) * power
            if last:
                outs[0][color] = value
                continue
            which, to = (color, g) if step < 2 else (0, g * 2 + color)
            peak = jnp.max(jnp.abs(value), axis=0, keepdims=True)
            power = jnp.floor(jnp.log2(jnp.maximum(peak, 2.0**-126)) * 64.0) + 2.0
            powers[which, pl.ds(to, 1), :] = power
            value = value * jnp.exp2(power * (-1.0 / 64)) * STEPS16
            outs[which][to * BINS : (to + 1) * BINS, :] = to_int16(value)
    if last:
        sub = lax.broadcasted_iota(jnp.int32, (SUB, lanes), 0)
        place = sub * lanes + lax.broadcasted_iota(jnp.int32, (SUB, lanes), 1)
        for d in range(2):
            p = plan.position(mine, 0, me, d)
            outs[1][d] = jnp.sum(jnp.where(place == p, live, 0.0))
        return
    whole = live.astype(jnp.int32)
    high = whole // LIVE_BASE
    pair = jnp.concatenate([whole - high * LIVE_BASE, high], axis=0).astype(jnp.int16)
    n = plan.count(step)
    tail = round_up(n, PACK)
    for which in range(2 if step < 2 else 1):
        out = outs[which]
        out[n * BINS : n * BINS + tail, :] = (
            powers[which, :tail, :].astype(jnp.int32).astype(jnp.int16)
        )
        out[n * BINS + tail : n * BINS + tail + PACK, :] = pair


def exchange(plan, step, arrays):
    lanes = arrays[0].shape[-1]
    coded = min(step, 2) * 2 + max(step - 2, 0)
    if step == plan.bits:
        out_shape = (
            jax.ShapeDtypeStruct((2, BINS, lanes), jnp.float32),
            jax.ShapeDtypeStruct((2,), jnp.float32),
        )
        out_specs = (VMEM, SMEM)
    else:
        out_shape = [jax.ShapeDtypeStruct((plan.rows(step), lanes), jnp.int16)]
        if step < 2:
            out_shape = out_shape * 2
        if step == 0:
            out_shape = out_shape + [jax.ShapeDtypeStruct((SUB, lanes), jnp.float32)]
        out_specs = [VMEM] * len(out_shape)
    tail = max(round_up(plan.count(a), PACK) for a in range(plan.bits))
    return pl.pallas_call(
        functools.partial(exchange_kernel, plan, step, lanes),
        out_shape=tuple(out_shape),
        in_specs=[VMEM] * len(arrays),
        out_specs=tuple(out_specs),
        scratch_shapes=[pltpu.VMEM((2 + coded, tail, lanes), jnp.float32)],
        compiler_params=pltpu.CompilerParams(vmem_limit_bytes=16 * MIB),
    )(*arrays)


def cold_kernel(plan, pay, out, stage, sem):
    lanes = out.shape[-1]
    sub = lax.broadcasted_iota(jnp.int32, (SUB, lanes), 0)
    unit = LIMIT / STEPS16

    def copies(o):
        at = pl.ds(o * plan.cap, plan.cap)
        return pltpu.make_async_copy(stage.at[o % 2], out.at[at], sem.at[o % 2])

    for o in range(plan.shards):
        if o >= 2:
            copies(o - 2).wait()
        tally = pay[o, plan.count_at : plan.pay_rows, :].astype(jnp.int32)
        for c in range(plan.cap):
            if c % 2 == 0:
                at = plan.sum_at + c * SUB
                means = pay[o, at : at + PACK, :].astype(jnp.float32) * unit
            count = jnp.broadcast_to(tally[c : c + 1, :], (SUB, lanes))
            n = jnp.clip(count - MINUTE * sub, 0, MINUTE).astype(jnp.float32)
            filled = n > 0
            ends = pay[o, c * 2 * SUB : (c + 1) * 2 * SUB, :].astype(jnp.float32) * unit
            stage[o % 2, c, 0] = jnp.where(filled, ends[:SUB], 0.0)
            stage[o % 2, c, 1] = jnp.where(filled, ends[SUB:], 0.0)
            stage[o % 2, c, 2] = means[(c % 2) * SUB : (c % 2 + 1) * SUB] * n
            stage[o % 2, c, 3] = n
        copies(o).start()
    for o in range(max(0, plan.shards - 2), plan.shards):
        copies(o).wait()


def cold(plan, pay, minutes):
    shards, _, lanes = pay.shape
    return pl.pallas_call(
        functools.partial(cold_kernel, plan),
        out_shape=jax.ShapeDtypeStruct((shards * plan.cap, 4, minutes, lanes), jnp.float32),
        in_specs=[VMEM],
        out_specs=ANY,
        scratch_shapes=[
            pltpu.VMEM((2, plan.cap, 4, minutes, lanes), jnp.float32),
            pltpu.SemaphoreType.DMA((2,)),
        ],
        compiler_params=pltpu.CompilerParams(vmem_limit_bytes=8 * MIB),
        name="cold",
    )(pay)


def body(samples, counts, buckets, series, omap):
    blocks, rows, _ = samples.shape
    plan = Plan(lax.axis_size("shard"), lax.axis_size("replica"), omap.shape[0], blocks)

    def swap(bit, x):
        return lax.ppermute(x, *plan.partner(bit))

    send, keep, send_near, keep_near = sketch(plan, samples, counts, buckets, series, omap)
    far = [keep, swap(-1, send)]
    near = [keep_near, swap(-1, send_near)]
    *sent, live = exchange(plan, 0, far)
    bits = [order[0] for order in plan.orders]
    coded = [swap(bits[color], sent[color]) for color in range(2)]
    pay = minute_stats(plan, samples, counts, series, omap, live)
    pay = lax.all_to_all(pay, "shard", split_axis=0, concat_axis=0, tiled=True)
    for step in range(1, plan.bits):
        sent = exchange(plan, step, [*near, *coded, live])
        bits = [order[step] for order in plan.orders]
        coded += [swap(bits[i], x) for i, x in enumerate(sent)]
    sketches, live_rows = exchange(plan, plan.bits, [*near, *coded, live])
    stats = cold(plan, pay, rows // MINUTE)
    return stats.reshape((1, 1) + stats.shape), sketches, live_rows


def solution(mesh):
    both = ("shard", "replica")
    return jax.shard_map(
        body,
        mesh=mesh,
        in_specs=(P(both, None, None), P(both), P(both, None), P(both), P()),
        out_specs=(
            P("shard", "replica", None, None, None, None),
            P(both, None, None),
            P(both),
        ),
        check_vma=False,
    )
```

time: 318 us -> 74.2 us (0.23)
  waiting for transfers between devices: 188 us -> 24.9 us
  matrix products: 32.9 us -> 0 us
  Pallas kernels: 0 us -> 28.3 us
  other arithmetic: 25.6 us -> 0 us
  local copies, waits for them, and re-layouts: 26.5 us -> 1.83 us
  between operations: 14.2 us -> 0.74 us
  blocking collectives: 6.8 us -> 0 us
  starting transfers between devices: 23 us -> 18.3 us
    all_to_all x4 -> x1, waiting for transfers between devices: 186 us -> 0.01 us  [body(): pay = lax.all_to_all(pay, 'shard', split_axis=0, concat_axis=0, tiled=True)]
    dot_general x3 -> x0, matrix products: 32.9 us -> none  [the longest x1 18.5 us: bucket_sketch(): jnp.einsum('nks,nsl->nkl', table, values, preferred_element_type=jnp.floa...]
    pallas_call x0 -> x8, Pallas kernels: none -> 28.3 us  [the longest x1 13.8 us: minute_stats(): pl.pallas_call(functools.partial(stats_kernel, plan), out_shape=jax.Shape...]
    ppermute x0 -> x8, waiting for transfers between devices: none -> 24.9 us  [swap(): return lax.ppermute(x, *plan.partner(bit))]
    all_to_all x4 -> x1, starting transfers between devices: 22.9 us -> 7.3 us  [body(): pay = lax.all_to_all(pay, 'shard', split_axis=0, concat_axis=0, tiled=True)]
    select_n x6 -> x0, other arithmetic: 14.9 us -> none  [the longest x1 12.3 us: body(): sketch_buf = jnp.where(used[:, None, None], sketch_all[source], 0.0)]
    ppermute x0 -> x8, starting transfers between devices: none -> 11 us  [swap(): return lax.ppermute(x, *plan.partner(bit))]
    gather x5 -> x0, local copies, waits for them, and re-layouts: 10.9 us -> none  [the longest x1 6.49 us: body(): sketch_buf = jnp.where(used[:, None, None], sketch_all[source], 0.0)]
  transfers between devices with their start and end apart: 5 -> 9, of which waited for: 3 -> 7; matrix products, arithmetic and copies ran while one was open for 25% -> 0% of each run, Pallas kernels for 0% -> 2%
where the time goes in v2:
time: 74.2 us; the launch traced here: 74 us
  Pallas kernels  28.3 us (38%)
  waiting for transfers between devices  24.9 us (34%)
  starting transfers between devices  18.3 us (25%)
  local copies, waits for them, and re-layouts  1.83 us (2%)
    ppermute x8, waiting for transfers between devices, swap(): return lax.ppermute(x, *plan.partner(bit))  24.9 us
    pallas_call x1, Pallas kernels, minute_stats(): pl.pallas_call(functools.partial(stats_kernel, plan), out_shape=jax.Shape...  13.8 us
    ppermute x8, starting transfers between devices, swap(): return lax.ppermute(x, *plan.partner(bit))  11 us
    pallas_call x1, Pallas kernels, sketch(): pl.pallas_call(functools.partial(sketch_kernel, plan, chunk), out_shape=(...  9.62 us
    all_to_all x1, starting transfers between devices, body(): pay = lax.all_to_all(pay, 'shard', split_axis=0, concat_axis=0, tiled=True)  7.3 us
    pallas_call x1, Pallas kernels, cold(): pl.pallas_call(functools.partial(cold_kernel, plan), out_shape=jax.ShapeD...  3.09 us
    unnamed x10, local copies, waits for them, and re-layouts  1.83 us
    pallas_call x5, Pallas kernels, exchange(): pl.pallas_call(functools.partial(exchange_kernel, plan, step, lanes), out...  1.8 us
  transfers between devices with their start and end apart: 9, of which 7 were waited for; matrix products, arithmetic and copies ran while one was open for 0% of the time, Pallas kernels for 2%

profile of v2, /device:TPU:0, one launch (start us, length us, event | category | flops | bytes accessed | tf_op | source)
XLA Modules:
  0.0 74.0 jit_solution(5624561428721543855)
XLA Ops:
  0.6 9.6 %sketch.1 = (f32[2056,128]{1,0:T(8,128)}, f32[2056,128]{1,0:T(8,128)}, f32[2048,128]{1,0:T(8,128)}, f32[2048,128]{1,0:T(8,128)}) custom-call(s32[64]{0:T(128)} %counts.3, s32[64]{0:T(128)} %series.3, s32[64]{0:T(128)} %omap.3, s32[64,480]{1,0:T(8,128)} %buckets.1, bf16[64,480,128]{2,1,0:T(8,128)(2,1)} %samples.3), custom_call_target="tpu_custom_call" | custom-call | tf_op jit(solution)/shard_map/sketch/pallas_call | solution.py:188
  10.3 0.6 collective-permute-start
  10.8 2.5 %collective-permute-done.refs_1_ = f32[2056,128]{1,0:T(8,128)S(1)} collective-permute-done((f32[2056,128]{1,0:T(8,128)}, f32[2056,128]{1,0:T(8,128)S(1)}, u32[]{:S(2)}, u32[]{:S(2)}) %collective-permute-start) | collective-permute-done | bytes 1052704 | tf_op jit(solution)/shard_map/ppermute | solution.py:471
  13.3 0.0 copy-start.1
  13.3 1.2 %copy-done.1 = f32[2056,128]{1,0:T(8,128)S(1)} copy-done((f32[2056,128]{1,0:T(8,128)S(1)}, f32[2056,128]{1,0:T(8,128)}, u32[]{:S(2)}) %copy-start.1) | copy-done | bytes 1052696
  14.5 0.4 shard_map.76
  15.0 0.0 copy-start.2
  15.0 0.6 copy-done.2
  15.6 0.0 copy-start.4
  15.6 13.8 %minute_stats.1 = s16[8,400,128]{2,1,0:T(8,128)(2,1)} custom-call(s32[64]{0:T(128)} %counts.3, s32[64]{0:T(128)} %series.3, s32[64]{0:T(128)} %omap.3, bf16[64,480,128]{2,1,0:T(8,128)(2,1)} %samples.3, f32[8,128]{1,0:T(8,128)} %copy-done.2), custom_call_target="tpu_custom_call" | custom-call | tf_op jit(solution)/shard_map/minute_stats/pallas_call | solution.py:303
  29.3 0.0 copy-start
  29.3 0.0 copy-start.3
  29.4 7.3 %all-to-all-start = ((s16[8,400,128]{2,1,0:T(8,128)(2,1)}), s16[8,400,128]{2,1,0:T(8,128)(2,1)S(1)}, u32[]{:S(2)}, u32[]{:S(2)}) async-start(s16[8,400,128]{2,1,0:T(8,128)(2,1)} %minute_stats.1), calls=%async_computation | async-start | bytes 1638400 | tf_op jit(solution)/shard_map/all_to_all | solution.py:480
  36.7 0.0 copy-done.4
  36.7 0.1 collective-permute-start.1
  36.7 1.6 %collective-permute-start.2 = (s16[1056,128]{1,0:T(8,128)(2,1)S(1)}, s16[1056,128]{1,0:T(8,128)(2,1)S(1)}, u32[]{:S(2)}, u32[]{:S(2)}) collective-permute-start(s16[1056,128]{1,0:T(8,128)(2,1)S(1)} %get-tuple-element.19), channel_id=1, source_target_pairs={{0,2},{1,3},{2,0},{3,1},{4,6},{5,7},{6,4},{7,5},{8,10},{9,11},{10,... | collective-permute-start | bytes 811016 | tf_op jit(solution)/shard_map/ppermute | solution.py:471
  38.3 1.9 %collective-permute-start.3 = (s16[1056,128]{1,0:T(8,128)(2,1)S(1)}, s16[1056,128]{1,0:T(8,128)(2,1)S(1)}, u32[]{:S(2)}, u32[]{:S(2)}) collective-permute-start(s16[1056,128]{1,0:T(8,128)(2,1)S(1)} %get-tuple-element.20), channel_id=1, source_target_pairs={{0,4},{4,0},{8,12},{12,8},{16,20},{20,16},{24,28},{28,24},{1,5},{5... | collective-permute-start | bytes 811016 | tf_op jit(solution)/shard_map/ppermute | solution.py:471
  40.3 0.0 collective-permute-done.1.refs_1_
  40.3 5.3 %collective-permute-done.2.refs_2_ = s16[1056,128]{1,0:T(8,128)(2,1)S(1)} collective-permute-done((s16[1056,128]{1,0:T(8,128)(2,1)S(1)}, s16[1056,128]{1,0:T(8,128)(2,1)S(1)}, u32[]{:S(2)}, u32[]{:S(2)}) %collective-permute-start.2) | collective-permute-done | bytes 270368 | tf_op jit(solution)/shard_map/ppermute | solution.py:471
  45.6 8.1 %collective-permute-done.3.refs_3_ = s16[1056,128]{1,0:T(8,128)(2,1)S(1)} collective-permute-done((s16[1056,128]{1,0:T(8,128)(2,1)S(1)}, s16[1056,128]{1,0:T(8,128)(2,1)S(1)}, u32[]{:S(2)}, u32[]{:S(2)}) %collective-permute-start.3) | collective-permute-done | bytes 270368 | tf_op jit(solution)/shard_map/ppermute | solution.py:471
  53.7 0.0 copy-done
  53.7 0.0 copy-done.3
  53.7 0.3 shard_map.77
  54.0 0.1 collective-permute-start.4
  54.1 1.6 %collective-permute-start.5 = (s16[544,128]{1,0:T(8,128)(2,1)S(1)}, s16[544,128]{1,0:T(8,128)(2,1)S(1)}, u32[]{:S(2)}, u32[]{:S(2)}) collective-permute-start(s16[544,128]{1,0:T(8,128)(2,1)S(1)} %get-tuple-element.22), channel_id=1, source_target_pairs={{0,2},{1,3},{2,0},{3,1},{4,6},{5,7},{6,4},{7,5},{8,10},{9,11},{10,... | collective-permute-start | bytes 417800 | tf_op jit(solution)/shard_map/ppermute | solution.py:471
  55.6 3.5 %collective-permute-done.4.refs_4_ = s16[544,128]{1,0:T(8,128)(2,1)S(1)} collective-permute-done((s16[544,128]{1,0:T(8,128)(2,1)S(1)}, s16[544,128]{1,0:T(8,128)(2,1)S(1)}, u32[]{:S(2)}, u32[]{:S(2)}) %collective-permute-start.4) | collective-permute-done | bytes 139296 | tf_op jit(solution)/shard_map/ppermute | solution.py:471
  59.1 0.1 collective-permute-done.5.refs_5_
  59.2 0.2 shard_map.78
  59.4 2.2 %collective-permute-start.6 = (s16[544,128]{1,0:T(8,128)(2,1)S(1)}, s16[544,128]{1,0:T(8,128)(2,1)S(1)}, u32[]{:S(2)}, u32[]{:S(2)}) collective-permute-start(s16[544,128]{1,0:T(8,128)(2,1)S(1)} %shard_map.78), channel_id=1, source_target_pairs={{0,8},{4,12},{8,0},{12,4},{16,24},{20,28},{24,16},{28,20},{1,9},{5... | collective-permute-start | bytes 417800 | tf_op jit(solution)/shard_map/ppermute | solution.py:471
  61.6 3.0 %collective-permute-done.6.refs_6_ = s16[544,128]{1,0:T(8,128)(2,1)S(1)} collective-permute-done((s16[544,128]{1,0:T(8,128)(2,1)S(1)}, s16[544,128]{1,0:T(8,128)(2,1)S(1)}, u32[]{:S(2)}, u32[]{:S(2)}) %collective-permute-start.6) | collective-permute-done | bytes 139296 | tf_op jit(solution)/shard_map/ppermute | solution.py:471
  64.6 0.1 shard_map.79
  64.8 3.0 %collective-permute-start.7 = (s16[288,128]{1,0:T(8,128)(2,1)S(1)}, s16[288,128]{1,0:T(8,128)(2,1)S(1)}, u32[]{:S(2)}, u32[]{:S(2)}) collective-permute-start(s16[288,128]{1,0:T(8,128)(2,1)S(1)} %shard_map.79), channel_id=1, source_target_pairs={{0,16},{4,20},{8,24},{12,28},{16,0},{20,4},{24,8},{28,12},{1,17},{... | collective-permute-start | bytes 221192 | tf_op jit(solution)/shard_map/ppermute | solution.py:471
  67.8 2.3 %collective-permute-done.7.refs_7_ = s16[288,128]{1,0:T(8,128)(2,1)S(1)} collective-permute-done((s16[288,128]{1,0:T(8,128)(2,1)S(1)}, s16[288,128]{1,0:T(8,128)(2,1)S(1)}, u32[]{:S(2)}, u32[]{:S(2)}) %collective-permute-start.7) | collective-permute-done | bytes 73760 | tf_op jit(solution)/shard_map/ppermute | solution.py:471
  70.1 0.8 %shard_map.80 = (f32[2,128,128]{2,1,0:T(8,128)}, f32[2]{0:T(128)}) custom-call(f32[2048,128]{1,0:T(8,128)S(1)} %copy-done, f32[2048,128]{1,0:T(8,128)S(1)} %collective-permute-done.1.refs_1_, s16[1056,128]{1,0:T(8,128)(2,1)S(1)} %collective-permute-done.2.refs_2_, s16[1056,128]{1,0:T(8,128)(2,1)S(1)} %collective-permute-done.3.refs_3_, ...), custom_call_target="tpu_custom_call" | custom-call | tf_op jit(solution)/shard_map/pallas_call | solution.py:410
  70.9 0.0 all-to-all-done.pay
  70.9 3.1 %cold.1 = f32[128,4,8,128]{3,2,1,0:T(8,128)} custom-call(s16[8,400,128]{2,1,0:T(8,128)(2,1)S(1)} %all-to-all-done.pay), custom_call_target="tpu_custom_call" | custom-call | tf_op jit(solution)/shard_map/cold/pallas_call | solution.py:452
Async XLA Ops:
  10.3 3.1 %collective-permute-start = (f32[2056,128]{1,0:T(8,128)}, f32[2056,128]{1,0:T(8,128)S(1)}, u32[]{:S(2)}, u32[]{:S(2)}) collective-permute-start(f32[2056,128]{1,0:T(8,128)} %get-tuple-element.15), channel_id=1, source_target_pairs={{0,1},{1,0},{2,3},{3,2},{4,5},{5,4},{6,7},{7,6},{8,9},{9,8},{10,11... | collective-permute-start | bytes 3158024 | tf_op jit(solution)/shard_map/ppermute | solution.py:471
  13.3 1.2 %copy-start.1 = (f32[2056,128]{1,0:T(8,128)S(1)}, f32[2056,128]{1,0:T(8,128)}, u32[]{:S(2)}) copy-start(f32[2056,128]{1,0:T(8,128)} %get-tuple-element.14.refs_0_) | copy-start | bytes 3158020
  15.0 0.6 copy-start.2
  15.6 21.1 %copy-start.4 = (f32[2048,128]{1,0:T(8,128)S(1)}, f32[2048,128]{1,0:T(8,128)}, u32[]{:S(2)}) copy-start(f32[2048,128]{1,0:T(8,128)} %get-tuple-element.18) | copy-start | bytes 3145732
  29.3 24.4 %copy-start = (f32[2048,128]{1,0:T(8,128)S(1)}, f32[2048,128]{1,0:T(8,128)}, u32[]{:S(2)}) copy-start(f32[2048,128]{1,0:T(8,128)} %get-tuple-element.17.refs_0_) | copy-start | bytes 3145732
  29.3 24.4 %copy-start.3 = (f32[8,128]{1,0:T(8,128)S(1)}, f32[8,128]{1,0:T(8,128)}, u32[]{:S(2)}) copy-start(f32[8,128]{1,0:T(8,128)} %copy-done.2) | copy-start | bytes 12292
  29.4 41.5 %all-to-all-start = ((s16[8,400,128]{2,1,0:T(8,128)(2,1)}), s16[8,400,128]{2,1,0:T(8,128)(2,1)S(1)}, u32[]{:S(2)}, u32[]{:S(2)}) async-start(s16[8,400,128]{2,1,0:T(8,128)(2,1)} %minute_stats.1), calls=%async_computation | async-start | bytes 1638400 | tf_op jit(solution)/shard_map/all_to_all | solution.py:480
  36.7 3.6 %collective-permute-start.1 = (f32[2048,128]{1,0:T(8,128)S(1)}, f32[2048,128]{1,0:T(8,128)S(1)}, u32[]{:S(2)}, u32[]{:S(2)}) collective-permute-start(f32[2048,128]{1,0:T(8,128)S(1)} %copy-done.4), channel_id=1, source_target_pairs={{0,1},{1,0},{2,3},{3,2},{4,5},{5,4},{6,7},{7,6},{8,9},{9,8},{10,11... | collective-permute-start | bytes 3145736 | tf_op jit(solution)/shard_map/ppermute | solution.py:471
  36.7 8.9 %collective-permute-start.2 = (s16[1056,128]{1,0:T(8,128)(2,1)S(1)}, s16[1056,128]{1,0:T(8,128)(2,1)S(1)}, u32[]{:S(2)}, u32[]{:S(2)}) collective-permute-start(s16[1056,128]{1,0:T(8,128)(2,1)S(1)} %get-tuple-element.19), channel_id=1, source_target_pairs={{0,2},{1,3},{2,0},{3,1},{4,6},{5,7},{6,4},{7,5},{8,10},{9,11},{10,... | collective-permute-start | bytes 811016 | tf_op jit(solution)/shard_map/ppermute | solution.py:471
  38.3 15.4 %collective-permute-start.3 = (s16[1056,128]{1,0:T(8,128)(2,1)S(1)}, s16[1056,128]{1,0:T(8,128)(2,1)S(1)}, u32[]{:S(2)}, u32[]{:S(2)}) collective-permute-start(s16[1056,128]{1,0:T(8,128)(2,1)S(1)} %get-tuple-element.20), channel_id=1, source_target_pairs={{0,4},{4,0},{8,12},{12,8},{16,20},{20,16},{24,28},{28,24},{1,5},{5... | collective-permute-start | bytes 811016 | tf_op jit(solution)/shard_map/ppermute | solution.py:471
  54.0 5.1 %collective-permute-start.4 = (s16[544,128]{1,0:T(8,128)(2,1)S(1)}, s16[544,128]{1,0:T(8,128)(2,1)S(1)}, u32[]{:S(2)}, u32[]{:S(2)}) collective-permute-start(s16[544,128]{1,0:T(8,128)(2,1)S(1)} %get-tuple-element.21), channel_id=1, source_target_pairs={{0,4},{4,0},{8,12},{12,8},{16,20},{20,16},{24,28},{28,24},{1,5},{5... | collective-permute-start | bytes 417800 | tf_op jit(solution)/shard_map/ppermute | solution.py:471
  54.1 5.1 %collective-permute-start.5 = (s16[544,128]{1,0:T(8,128)(2,1)S(1)}, s16[544,128]{1,0:T(8,128)(2,1)S(1)}, u32[]{:S(2)}, u32[]{:S(2)}) collective-permute-start(s16[544,128]{1,0:T(8,128)(2,1)S(1)} %get-tuple-element.22), channel_id=1, source_target_pairs={{0,2},{1,3},{2,0},{3,1},{4,6},{5,7},{6,4},{7,5},{8,10},{9,11},{10,... | collective-permute-start | bytes 417800 | tf_op jit(solution)/shard_map/ppermute | solution.py:471
  59.4 5.2 %collective-permute-start.6 = (s16[544,128]{1,0:T(8,128)(2,1)S(1)}, s16[544,128]{1,0:T(8,128)(2,1)S(1)}, u32[]{:S(2)}, u32[]{:S(2)}) collective-permute-start(s16[544,128]{1,0:T(8,128)(2,1)S(1)} %shard_map.78), channel_id=1, source_target_pairs={{0,8},{4,12},{8,0},{12,4},{16,24},{20,28},{24,16},{28,20},{1,9},{5... | collective-permute-start | bytes 417800 | tf_op jit(solution)/shard_map/ppermute | solution.py:471
  64.8 5.3 %collective-permute-start.7 = (s16[288,128]{1,0:T(8,128)(2,1)S(1)}, s16[288,128]{1,0:T(8,128)(2,1)S(1)}, u32[]{:S(2)}, u32[]{:S(2)}) collective-permute-start(s16[288,128]{1,0:T(8,128)(2,1)S(1)} %shard_map.79), channel_id=1, source_target_pairs={{0,16},{4,20},{8,24},{12,28},{16,0},{20,4},{24,8},{28,12},{1,17},{... | collective-permute-start | bytes 221192 | tf_op jit(solution)/shard_map/ppermute | solution.py:471
